TPU v7x, 32 devices: a whole 2x2x4 slice. The times are simulated.
32 devices in a mesh: pts: 8 (over z, y), feat: 4 (over x, core).
Axes of the slice: x: 2, y: 2, z: 4, core: 2. Of those that a mesh axis runs over, the one named last changes fastest.
Arguments:
- slab: bfloat16 [16384, 768], P('pts', 'feat'), may hold values from -40 to 40
- centres: bfloat16 [4096, 768], replicated, may hold values from -3 to 3
- labels: int32 [16384, 1], P(('pts', 'feat')), may hold values from 0 to 4095
- sample_rows: int32 [8, 8, 4], P('pts'), may hold values from 0 to 2047, as said below
- sample_count: int32 [8, 8], P('pts'), may hold values from 0 to 4, as said below
- slot_offset: int32 [8, 8], P('pts'), may hold values from 0 to 28, as said below
Outputs:
- coreset: bfloat16 [256, 768], P('pts', 'feat')
Inputs may be any that keep to these rules, and one draw needn't show every extreme that they name: `sample_rows`: row indices within a source shard; sampled independently with replacement. `sample_count`: in every draw some owner receives 4 rows from every source. slot_offset[o,p] is the sum of sample_count[q,o] over sources q < p.
All inputs are finite; a program needn't handle non-finite values.
Results may differ from a plain program's by a relative error of at most 0.0006.
Values may be sent and summed in bfloat16 or wider, within the bound.
A program may use at most 64 MiB of HBM per device.

v0:
```python
import jax
import jax.numpy as jnp
from jax import lax
from jax.sharding import PartitionSpec as P


def local(slab, centres, labels, sample_rows, sample_count, slot_offset):
    rows_pts, feat_width = slab.shape
    feat_count = lax.axis_size("feat")
    rows_dev = rows_pts // feat_count
    centre_count = centres.shape[0]
    contract = (((1,), (1,)), ((), ()))
    centre_sq = jnp.sum(jnp.square(centres.astype(jnp.float32)), axis=1)
    stacked = slab.reshape(feat_count, rows_dev, feat_width)
    points = lax.all_to_all(stacked, "feat", split_axis=0, concat_axis=2, tiled=True)[0]
    cross_term = lax.dot_general(points, centres, contract, preferred_element_type=jnp.float32)
    point_sq = jnp.sum(jnp.square(points.astype(jnp.float32)), axis=1)
    nearest = jnp.min(point_sq[:, None] + centre_sq[None, :] - 2.0 * cross_term, axis=1)[None, :][0]
    member = labels[:, 0]
    cost_part = jax.ops.segment_sum(nearest, member, num_segments=centre_count)
    size_part = jax.ops.segment_sum(jnp.ones_like(nearest), member, num_segments=centre_count)
    cluster_cost, cluster_size = lax.psum((cost_part, size_part), ("pts", "feat"))
    own_sens = nearest / jnp.take(cluster_cost, member) + 1.0 / jnp.take(cluster_size, member)
    shard_sens = lax.all_gather(own_sens, "feat", axis=0, tiled=True)
    total_points = rows_pts * lax.axis_size("pts")
    weight = 2.0 * centre_count / total_points / shard_sens
    picked_rows = sample_rows[0]
    owner_count, slot_count = picked_rows.shape
    chosen = jnp.take(slab, picked_rows.reshape(-1), axis=0).reshape(
        owner_count, slot_count, feat_width
    )
    chosen_weight = jnp.take(weight, picked_rows)
    live_slot = jnp.arange(slot_count, dtype=jnp.int32)[None, :] < sample_count[0][:, None]
    scaled = jnp.where(
        live_slot[:, :, None], chosen.astype(jnp.float32) * chosen_weight[:, :, None], 0.0
    ).astype(jnp.bfloat16)
    arrived = lax.all_to_all(scaled, "pts", split_axis=0, concat_axis=0, tiled=True)
    target = slot_offset[0][:, None] + jnp.arange(slot_count, dtype=jnp.int32)[None, :]
    own_rows = arrived.shape[0] * slot_count
    placed = jnp.zeros((own_rows, feat_width), jnp.float32)
    placed = placed.at[target.reshape(-1)].add(
        arrived.reshape(-1, feat_width).astype(jnp.float32), mode="drop"
    )
    return placed.astype(jnp.bfloat16)


def solution(mesh):
    placed = (
        P("pts", "feat"),
        P(),
        P(("pts", "feat"), None),
        P("pts", None, None),
        P("pts", None),
        P("pts", None),
    )
    return jax.shard_map(
        local, mesh=mesh, in_specs=placed, out_specs=P("pts", "feat"), check_vma=False
    )
```

profile of v0, /device:TPU:0, one launch (start us, length us, event | category | flops | bytes accessed | tf_op | source)
XLA Modules:
  0.0 99.5 jit_solution(1397401444950790253)
XLA Ops:
  0.0 2.1 %copy.35 = bf16[24,4,8,512]{3,2,0,1:T(8,128)(2,1)} copy(bf16[24,4,8,512]{3,2,1,0:T(8,128)(2,1)} %bitcast.31) | data formatting | bytes 1572864 | tf_op jit(solution)/shard_map/reshape | solution.py:14
  2.1 4.2 %all-to-all-start = ((bf16[4,512,192]{1,2,0:T(8,128)(2,1)}), bf16[4,512,192]{1,2,0:T(8,128)(2,1)S(1)}, u32[]{:S(2)}, u32[]{:S(2)}) async-start(bf16[4,512,192]{1,2,0:T(8,128)(2,1)} %bitcast.29), calls=%async_computation | async-start | bytes 1572864 | tf_op jit(solution)/shard_map/all_to_all | solution.py:15
  6.3 1.4 %copy.28 = bf16[2048,192]{1,0:T(8,128)(2,1)S(1)} copy(bf16[2048,192]{0,1:T(8,128)(2,1)} %param.8) | data formatting | bytes 1572864 | tf_op args[0]
  7.8 0.7 compare_select_fusion.1
  8.4 0.8 copy.27
  9.2 0.7 compare_select_fusion
  9.9 0.1 copy.30
  10.0 0.1 reshape.185
  10.1 0.1 reshape_squeeze.6
  10.2 0.6 gather_fusion
  10.8 0.7 iota_compare_fusion
  11.5 0.7 iota_add_fusion
  12.3 0.1 add.119
  12.3 3.4 %scatter_custom_fusion.1 = f32[4096]{0:T(1024)S(1)} fusion(s32[512]{0:T(512)} %bitcast.35, f32[512]{0:T(512)S(1)} %broadcast.113, f32[]{:T(128)} %constant.22.clone.1), kind=kCustom, calls=%fused_computation.14 | custom fusion | flops 512 | bytes 16896 | tf_op jit(solution)/shard_map/scatter-add | solution.py:21
  15.8 4.1 %multiply_reduce_fusion = f32[4096]{0:T(1024)S(1)} fusion(bf16[4096,768]{1,0:T(8,128)(2,1)} %param.9), kind=kLoop, calls=%fused_computation.7 | loop fusion | flops 9433088 | bytes 6307840 | tf_op jit(solution)/shard_map/reduce_sum | solution.py:13
  19.8 0.0 all-to-all-done
  19.9 0.2 multiply_reduce_fusion.1
  20.1 0.0 copy-start.1
  20.1 7.5 %subtract_reduce_fusion = f32[512]{0:T(512)S(1)} fusion(bf16[512,768]{0,1:T(8,128)(2,1)S(1)} %bitcast.32, bf16[4096,768]{1,0:T(8,128)(2,1)} %param.9, f32[4096]{0:T(1024)S(1)} %multiply_reduce_fusion, f32[512]{0:T(512)S(1)} %multiply_reduce_fusion.1), kind=kOutput, calls=%fused_computation.8 | convolution fusion | flops 3229613568 | bytes 7098368 | tf_op jit(solution)/shard_map/dot_general | solution.py:16
  27.6 0.0 copy-done.1
  27.6 0.0 copy-start
  27.6 3.3 %scatter_custom_fusion = f32[4096]{0:T(1024)S(1)} fusion(s32[512]{0:T(512)S(1)} %bitcast.36, f32[512]{0:T(512)S(1)} %subtract_reduce_fusion, f32[]{:T(128)} %constant.22.clone.1), kind=kCustom, calls=%fused_computation.16 | custom fusion | flops 512 | bytes 16388 | tf_op jit(solution)/shard_map/scatter-add | solution.py:20
  30.9 42.0 %all-reduce = (f32[4096]{0:T(1024)S(1)}, f32[4096]{0:T(1024)S(1)}) all-reduce(f32[4096]{0:T(1024)S(1)} %scatter_custom_fusion.1, f32[4096]{0:T(1024)S(1)} %scatter_custom_fusion), channel_id=1, replica_groups=mesh['pts'=8,'feat'=4] {'pts','feat'}, use_global_device_ids=true, to_apply=%region_6.8 | all-reduce | flops 8192 | bytes 65536 | tf_op jit(solution)/shard_map/psum | solution.py:22
  72.9 3.1 %gather_fusion.2 = f32[512]{0:T(512)S(1)} fusion(f32[4096]{0:T(1024)S(1)} %get-tuple-element.7, s32[1024]{0:T(1024)S(1)} %pad_clamp_fusion.1), kind=kCustom, calls=%fused_computation.clone | custom fusion | bytes 6144 | tf_op jit(solution)/shard_map/jit(_take)/gather | solution.py:23
  76.0 3.1 %gather_fusion.3 = f32[512]{0:T(512)S(1)} fusion(f32[4096]{0:T(1024)S(1)} %get-tuple-element.6, s32[1024]{0:T(1024)S(1)} %pad_clamp_fusion.1), kind=kCustom, calls=%fused_computation.1.clone | custom fusion | bytes 6144 | tf_op jit(solution)/shard_map/jit(_take)/gather | solution.py:23
  79.2 5.5 %all-gather = f32[4,1,512]{2,1,0:T(1,128)S(1)} all-gather(f32[1,1,512]{2,1,0:T(1,128)S(1)} %bitcast.33), channel_id=1, replica_groups=mesh['pts'=8,'feat'=4] {'feat'}, dimensions={0}, use_global_device_ids=true | all-gather | bytes 10240 | tf_op jit(solution)/shard_map/all_gather | solution.py:24
  84.7 0.7 gather_fusion.1
  85.4 0.1 reshape.184
  85.4 0.1 copy.31
  85.5 0.0 copy-done
  85.5 0.1 copy.32
  85.6 0.1 copy.26
  85.7 0.7 select_convert_fusion
  86.4 5.1 %all-to-all-start.1 = ((bf16[8,4,192]{2,1,0:T(4,128)(2,1)}), bf16[8,4,192]{2,1,0:T(4,128)(2,1)S(1)}, u32[]{:S(2)}, u32[]{:S(2)}) async-start(bf16[8,4,192]{2,1,0:T(4,128)(2,1)} %select_convert_fusion), calls=%async_computation.1 | async-start | bytes 32768 | tf_op jit(solution)/shard_map/all_to_all | solution.py:37
  91.5 6.6 %all-to-all-done.1 = bf16[8,4,192]{2,1,0:T(4,128)(2,1)S(1)} async-done(((bf16[8,4,192]{2,1,0:T(4,128)(2,1)}), bf16[8,4,192]{2,1,0:T(4,128)(2,1)S(1)}, u32[]{:S(2)}, u32[]{:S(2)}) %all-to-all-start.1) | async-done | bytes 12320 | tf_op jit(solution)/shard_map/all_to_all | solution.py:37
  98.1 0.8 scatter_custom_fusion.2
  98.9 0.6 convert_element_type.28
  (11 shorter events, 0.1 us)
Async XLA Ops:
  2.1 17.8 %all-to-all-start = ((bf16[4,512,192]{1,2,0:T(8,128)(2,1)}), bf16[4,512,192]{1,2,0:T(8,128)(2,1)S(1)}, u32[]{:S(2)}, u32[]{:S(2)}) async-start(bf16[4,512,192]{1,2,0:T(8,128)(2,1)} %bitcast.29), calls=%async_computation | async-start | bytes 1572864 | tf_op jit(solution)/shard_map/all_to_all | solution.py:15
  20.1 7.5 %copy-start.1 = (s32[512,1]{0,1:T(1,128)S(1)}, s32[512,1]{0,1:T(1,128)}, u32[]{:S(2)}) copy-start(s32[512,1]{0,1:T(1,128)} %param.10) | copy-start | bytes 6148
  27.6 57.9 %copy-start = (s32[1,8,4]{1,2,0:T(4,128)S(1)}, s32[1,8,4]{1,2,0:T(4,128)}, u32[]{:S(2)}) copy-start(s32[1,8,4]{1,2,0:T(4,128)} %param.11) | copy-start | bytes 388
  86.4 11.6 %all-to-all-start.1 = ((bf16[8,4,192]{2,1,0:T(4,128)(2,1)}), bf16[8,4,192]{2,1,0:T(4,128)(2,1)S(1)}, u32[]{:S(2)}, u32[]{:S(2)}) async-start(bf16[8,4,192]{2,1,0:T(4,128)(2,1)} %select_convert_fusion), calls=%async_computation.1 | async-start | bytes 32768 | tf_op jit(solution)/shard_map/all_to_all | solution.py:37
where the time goes:
time: 100 us; the launch traced here: 99.5 us
  blocking collectives  47.4 us (47%)
  other arithmetic  15.9 us (16%)
  local copies, waits for them, and re-layouts  12.6 us (13%)
  starting transfers between devices  9.3 us (9%)
  matrix products  7.52 us (8%)
  waiting for transfers between devices  6.57 us (7%)
    psum x1, blocking collectives, local(): lax.psum((cost_part, size_part), ('pts', 'feat'))  42 us
    dot_general x1, matrix products, local(): lax.dot_general(points, centres, contract, preferred_element_type=jnp.flo...  7.52 us
    all_to_all x1, waiting for transfers between devices, local(): lax.all_to_all(scaled, 'pts', split_axis=0, concat_axis=0, tiled=True)  6.57 us
    all_gather x1, blocking collectives, local(): shard_sens = lax.all_gather(own_sens, 'feat', axis=0, tiled=True)  5.45 us
    all_to_all x1, starting transfers between devices, local(): lax.all_to_all(scaled, 'pts', split_axis=0, concat_axis=0, tiled=True)  5.07 us
    all_to_all x1, starting transfers between devices, local(): lax.all_to_all(stacked, 'feat', split_axis=0, concat_axis=2, tiled=True)[0]  4.24 us
    reduce_sum x1, other arithmetic, local(): centre_sq = jnp.sum(jnp.square(centres.astype(jnp.float32)), axis=1)  4.09 us
    scatter-add x1, other arithmetic, local(): jax.ops.segment_sum(jnp.ones_like(nearest), member, num_segments=centre_c...  3.39 us
  transfers between devices with their start and end apart: 2, of which 1 were waited for; matrix products, arithmetic and copies ran while one was open for 14% of the time, Pallas kernels for 0%

commit v1 on v0

--- a/solution.py
+++ b/solution.py
@@ -1,7 +1,17 @@
+import functools
+
 import jax
 import jax.numpy as jnp
 from jax import lax
+from jax.experimental import pallas as pl
+from jax.experimental.pallas import tpu as pltpu
 from jax.sharding import PartitionSpec as P
+
+NT = (((1,), (1,)), ((), ()))
+LANES = 128
+HALF = LANES // 2
+SUB = 8
+MESH = pl.DeviceIdType.MESH
 
 
 def local(slab, centres, labels, sample_rows, sample_count, slot_offset):
@@ -9,11 +19,10 @@
     feat_count = lax.axis_size("feat")
     rows_dev = rows_pts // feat_count
     centre_count = centres.shape[0]
-    contract = (((1,), (1,)), ((), ()))
     centre_sq = jnp.sum(jnp.square(centres.astype(jnp.float32)), axis=1)
     stacked = slab.reshape(feat_count, rows_dev, feat_width)
     points = lax.all_to_all(stacked, "feat", split_axis=0, concat_axis=2, tiled=True)[0]
-    cross_term = lax.dot_general(points, centres, contract, preferred_element_type=jnp.float32)
+    cross_term = lax.dot_general(points, centres, NT, preferred_element_type=jnp.float32)
     point_sq = jnp.sum(jnp.square(points.astype(jnp.float32)), axis=1)
     nearest = jnp.min(point_sq[:, None] + centre_sq[None, :] - 2.0 * cross_term, axis=1)[None, :][0]
     member = labels[:, 0]
@@ -44,7 +53,288 @@
     return placed.astype(jnp.bfloat16)
 
 
+def kernel(n_p, n_f, chunks, tile, slab_ref, labels_ref, rows_ref, count_ref, offset_ref, cen_hbm,
+           out_ref, cen, csq, pack_a, pack_b, got_a, got_b, lab_msg, lab_all, row_msg, row_all,
+           red_msg, red_all, cen_sem, a_send, a_recv, b_send, b_recv, lab_send, lab_recv,
+           row_send, row_recv, red_send, red_recv):
+    f32, bf16 = jnp.float32, jnp.bfloat16
+    rows_pts, width = slab_ref.shape
+    rows_dev = rows_pts // n_f
+    crow = rows_dev // chunks
+    hrow = crow // 2
+    n = n_p * n_f
+    centre_count = cen.shape[0]
+    slots = rows_ref.shape[2]
+    tiles = centre_count // tile
+    my_p, my_f = lax.axis_index("pts"), lax.axis_index("feat")
+    me = my_p * n_f + my_f
+
+    def device(d):
+        other = lax.rem(me + d, n)
+        return other // n_f, lax.rem(other, n_f)
+
+    barrier = pltpu.get_barrier_semaphore()
+    for d in range(1, n):
+        pl.semaphore_signal(barrier, inc=1, device_id=device(d), device_id_type=MESH)
+
+    cen_copies = []
+    for t in range(tiles):
+        part = pl.ds(t * tile, tile)
+        copy = pltpu.make_async_copy(cen_hbm.at[part], cen.at[part], cen_sem.at[t])
+        copy.start()
+        cen_copies.append(copy)
+
+    odd = lax.rem(my_f, 2)
+
+    @pl.loop(0, n_f * chunks)
+    def _(j):
+        base = pl.multiple_of(j * crow, crow)
+        left = slab_ref[pl.ds(base, crow), :LANES].astype(f32)
+        right = slab_ref[pl.ds(base, crow), LANES:width].astype(f32)
+        right = jnp.concatenate([right, right], axis=1)
+        turned = pltpu.roll(left, HALF, 1)
+        low = lax.broadcasted_iota(jnp.int32, (crow, LANES), 1) < HALF
+        is_odd = jnp.full((crow, LANES), odd, jnp.int32) == 1
+        main = jnp.where(is_odd, jnp.where(low, turned, right), left)
+        rest = jnp.where(is_odd, jnp.where(low, left, turned), right)
+        pack_a[pl.ds(base, crow), :] = main.astype(bf16)
+        both = jnp.where(low[:hrow], rest[:hrow], rest[hrow:])
+        pack_b[pl.ds(pl.multiple_of(j * hrow, hrow), hrow), :] = both.astype(bf16)
+
+    pl.semaphore_wait(barrier, n - 1)
+
+    slab_copies = []
+    order = [e for e in range(2, n_f)] + [1]
+    for c in range(chunks):
+        copies = []
+        for e in order:
+            peer = lax.rem(my_f + e, n_f)
+            at = pl.multiple_of(peer * rows_dev + c * crow, crow)
+            half_at = pl.multiple_of(peer * (rows_dev // 2) + c * hrow, hrow)
+            copies.append(pltpu.make_async_remote_copy(
+                src_ref=pack_a.at[pl.ds(at, crow)], dst_ref=got_a.at[my_f, pl.ds(c * crow, crow)],
+                send_sem=a_send.at[c, e - 1], recv_sem=a_recv.at[c, e - 1],
+                device_id=(my_p, peer), device_id_type=MESH))
+            copies.append(pltpu.make_async_remote_copy(
+                src_ref=pack_b.at[pl.ds(half_at, hrow)], dst_ref=got_b.at[my_f, pl.ds(c * hrow, hrow)],
+                send_sem=b_send.at[c, e - 1], recv_sem=b_recv.at[c, e - 1],
+                device_id=(my_p, peer), device_id_type=MESH))
+        for copy in copies:
+            copy.start()
+        slab_copies.append(copies)
+    got_a[my_f] = pack_a[pl.ds(pl.multiple_of(my_f * rows_dev, rows_dev), rows_dev), :]
+    got_b[my_f] = pack_b[pl.ds(pl.multiple_of(my_f * (rows_dev // 2), rows_dev // 2), rows_dev // 2), :]
+
+    queries = n_p * SUB
+    query_sub = lax.broadcasted_iota(jnp.int32, (queries, 1), 0)
+    picked = jnp.full((queries, 1), -1, jnp.int32)
+    for o in range(n_p):
+        for s in range(slots):
+            picked = jnp.where(query_sub == o * SUB + s, rows_ref[0, o, s], picked)
+    members = labels_ref[...].astype(f32)
+    lane_dev = lax.broadcasted_iota(jnp.int32, (queries, rows_dev), 1)
+    own_hit = (lane_dev + my_f * rows_dev) == picked
+    own_label = jnp.sum(jnp.where(own_hit, members + 1.0, 0.0), axis=1, keepdims=True)
+    query_diag = (lax.broadcasted_iota(jnp.int32, (queries, LANES), 0)
+                  == lax.broadcasted_iota(jnp.int32, (queries, LANES), 1))
+    label_row = jnp.sum(jnp.where(query_diag, own_label, 0.0), axis=0, keepdims=True)
+    lab_msg[...] = label_row
+    lab_all[me] = label_row
+
+    lab_copies = []
+    for d in range(1, n):
+        copy = pltpu.make_async_remote_copy(
+            src_ref=lab_msg, dst_ref=lab_all.at[me], send_sem=lab_send.at[d - 1],
+            recv_sem=lab_recv.at[d - 1], device_id=device(d), device_id_type=MESH)
+        copy.start()
+        lab_copies.append(copy)
+
+    lane_pts = lax.broadcasted_iota(jnp.int32, (queries, rows_pts), 1)
+    chosen = jnp.where(lane_pts == picked, 1.0, 0.0).astype(bf16)
+    chosen = jnp.dot(chosen, slab_ref[...], preferred_element_type=f32)
+    live = jnp.zeros((queries, 1), f32)
+    for o in range(n_p):
+        for s in range(slots):
+            flag = jnp.where(count_ref[0, o] > s, 1.0, 0.0)
+            live = jnp.where(query_sub == o * SUB + slots + s, flag, live)
+    is_row = lax.rem(lax.broadcasted_iota(jnp.int32, (queries, width), 0), SUB) < slots
+    sent = jnp.where(is_row, chosen, live)
+    row_msg[:, :, :width] = sent.reshape(n_p, SUB, width)
+    row_all[my_p] = row_msg[my_p]
+    row_copies = []
+    for d in range(1, n_p):
+        owner = lax.rem(my_p + d, n_p)
+        copy = pltpu.make_async_remote_copy(
+            src_ref=row_msg.at[owner], dst_ref=row_all.at[my_p], send_sem=row_send.at[d - 1],
+            recv_sem=row_recv.at[d - 1], device_id=(owner, my_f), device_id_type=MESH)
+        copy.start()
+        row_copies.append(copy)
+
+    for t in range(tiles):
+        cen_copies[t].wait()
+
+    @pl.loop(0, tiles)
+    def _(t):
+        part = pl.ds(pl.multiple_of(t * tile, tile), tile)
+        total = jnp.zeros((tile, LANES), f32)
+        for b in range(cen.shape[1] // LANES):
+            piece = cen[part, b * LANES:(b + 1) * LANES].astype(f32)
+            total += piece * piece
+        csq[part, :] = jnp.broadcast_to(jnp.sum(total, axis=1, keepdims=True), (tile, LANES))
+
+    for copy in lab_copies:
+        copy.wait()
+    lanes = lax.broadcasted_iota(jnp.int32, (queries, LANES), 1)
+    slot = lax.rem(lax.broadcasted_iota(jnp.int32, (queries, LANES), 0), SUB)
+    is_slot = slot < slots
+    wanted = []
+    sums = jnp.zeros((queries, LANES), f32)
+    span = n_p * slots
+    for p in range(n_p):
+        row = lab_all[p * n_f]
+        for g in range(1, n_f):
+            row = row + lab_all[p * n_f + g]
+        want = jnp.sum(jnp.where(query_diag, row, 0.0), axis=1, keepdims=True) - 1.0
+        wanted.append(want)
+        size = jnp.sum(jnp.where(want == members, 1.0, 0.0), axis=1, keepdims=True)
+        sums = jnp.where(is_slot & (lanes == span + p * slots + slot), size, sums)
+
+    ones = jnp.ones((SUB, cen.shape[1]), bf16)
+    near_parts = []
+    for c in range(chunks):
+        for copy in slab_copies[c]:
+            copy.wait_recv()
+        rows = pl.ds(c * crow, crow)
+        half_rows = pl.ds(c * hrow, hrow)
+        low = lax.broadcasted_iota(jnp.int32, (hrow, LANES), 1) < HALF
+        blocks = []
+        for pair in range(n_f // 2):
+            even_b = got_b[2 * pair, half_rows].astype(f32)
+            odd_b = got_b[2 * pair + 1, half_rows].astype(f32)
+            top = jnp.where(low, even_b, pltpu.roll(odd_b, HALF, 1))
+            bottom = jnp.where(low, pltpu.roll(even_b, HALF, 1), odd_b)
+            middle = jnp.concatenate([top, bottom], axis=0).astype(bf16)
+            blocks += [got_a[2 * pair, rows], middle, got_a[2 * pair + 1, rows]]
+        points = jnp.concatenate(blocks, axis=1)
+        wide = points.astype(f32)
+        wide = wide * wide
+        high = wide.astype(bf16)
+        rest = (wide - high.astype(f32)).astype(bf16)
+        point_sq = (lax.dot_general(ones, high, NT, preferred_element_type=f32)
+                    + lax.dot_general(ones, rest, NT, preferred_element_type=f32))[:1]
+
+        def step(t, best):
+            part = pl.ds(pl.multiple_of(t * tile, tile), tile)
+            cross = lax.dot_general(cen[part, :], points, NT, preferred_element_type=f32)
+            square = csq[part, :]
+            gap = jnp.concatenate([square] * (crow // LANES), axis=1) - 2.0 * cross
+            return jnp.minimum(best, jnp.min(gap.reshape(tile // SUB, SUB, crow), axis=0))
+
+        best = lax.fori_loop(0, tiles, step, jnp.full((SUB, crow), jnp.inf, f32))
+        near_parts.append(point_sq + jnp.min(best, axis=0, keepdims=True))
+    nearest = jnp.concatenate(near_parts, axis=1)
+
+    for p in range(n_p):
+        cost = jnp.sum(jnp.where(wanted[p] == members, nearest, 0.0), axis=1, keepdims=True)
+        sums = jnp.where(is_slot & (lanes == p * slots + slot), cost, sums)
+    own_near = jnp.sum(jnp.where(own_hit, nearest, 0.0), axis=1, keepdims=True)
+    sums = jnp.where(is_slot & (lanes == 2 * span + my_p * slots + slot), own_near, sums)
+    to_owner = jnp.sum(jnp.where(is_slot, sums, 0.0).reshape(n_p, SUB, LANES), axis=1, keepdims=True)
+    red_msg[...] = to_owner
+    red_all[0] = red_msg[my_p]
+    red_copies = []
+    for d in range(1, n):
+        to = device(d)
+        copy = pltpu.make_async_remote_copy(
+            src_ref=red_msg.at[to[0]], dst_ref=red_all.at[d], send_sem=red_send.at[d - 1],
+            recv_sem=red_recv.at[d - 1], device_id=to, device_id_type=MESH)
+        copy.start()
+        red_copies.append(copy)
+    for copy in row_copies:
+        copy.wait()
+    for copies in slab_copies:
+        for copy in copies:
+            copy.wait_send()
+    for copy in red_copies:
+        copy.wait()
+    total = jnp.broadcast_to(jnp.sum(red_all[...], axis=0), (SUB, LANES))
+    size = pltpu.roll(total, LANES - span, 1)
+    near = pltpu.roll(total, LANES - 2 * span, 1)
+    weight = (2.0 * centre_count / (rows_pts * n_p)) / (near / total + 1.0 / size)
+    sub = lax.broadcasted_iota(jnp.int32, (SUB, LANES), 0)
+    lane = lax.broadcasted_iota(jnp.int32, (SUB, LANES), 1)
+    out_rows = out_ref.shape[0]
+    out_iota = lax.broadcasted_iota(jnp.int32, (out_rows, width), 0)
+    placed = jnp.zeros((out_rows, width), f32)
+    for p in range(n_p):
+        mine = (sub < slots) & (lane == p * slots + sub)
+        factor = jnp.sum(jnp.where(mine, weight, 0.0), axis=1, keepdims=True)
+        block = row_all[p][:, :width]
+        scaled = (block * factor).astype(bf16).astype(f32)
+        for s in range(slots):
+            flag = block[slots + s:slots + s + 1] > 0.5
+            hit = (out_iota == offset_ref[0, p] + s) & flag
+            placed = jnp.where(hit, scaled[s:s + 1], placed)
+    out_ref[...] = placed.astype(bf16)
+
+
+def fused(n_p, n_f, slab, centres, labels, sample_rows, sample_count, slot_offset):
+    rows_pts, width = slab.shape
+    rows_dev = rows_pts // n_f
+    centre_count, depth = centres.shape
+    slots = sample_rows.shape[2]
+    chunks = 2
+    tile = 512
+    tiles = centre_count // tile
+    n = n_p * n_f
+    wide = pl.cdiv(width, LANES) * LANES
+    vmem, smem = pl.BlockSpec(memory_space=pltpu.VMEM), pl.BlockSpec(memory_space=pltpu.SMEM)
+    dma = pltpu.SemaphoreType.DMA
+    return pl.pallas_call(
+        functools.partial(kernel, n_p, n_f, chunks, tile),
+        out_shape=jax.ShapeDtypeStruct((n_p * slots, width), jnp.bfloat16),
+        in_specs=[vmem, vmem, smem, smem, smem, pl.BlockSpec(memory_space=pl.ANY)],
+        out_specs=vmem,
+        scratch_shapes=[
+            pltpu.VMEM((centre_count, depth), jnp.bfloat16),
+            pltpu.VMEM((centre_count, LANES), jnp.float32),
+            pltpu.VMEM((rows_pts, LANES), jnp.bfloat16),
+            pltpu.VMEM((rows_pts // 2, LANES), jnp.bfloat16),
+            pltpu.VMEM((n_f, rows_dev, LANES), jnp.bfloat16),
+            pltpu.VMEM((n_f, rows_dev // 2, LANES), jnp.bfloat16),
+            pltpu.VMEM((1, LANES), jnp.float32),
+            pltpu.VMEM((n, 1, LANES), jnp.float32),
+            pltpu.VMEM((n_p, SUB, wide), jnp.float32),
+            pltpu.VMEM((n_p, SUB, wide), jnp.float32),
+            pltpu.VMEM((n_p, 1, LANES), jnp.float32),
+            pltpu.VMEM((n, 1, LANES), jnp.float32),
+            dma((tiles,)),
+            dma((chunks, n_f - 1)), dma((chunks, n_f - 1)),
+            dma((chunks, n_f - 1)), dma((chunks, n_f - 1)),
+            dma((n - 1,)), dma((n - 1,)),
+            dma((n_p - 1,)), dma((n_p - 1,)),
+            dma((n - 1,)), dma((n - 1,)),
+        ],
+        compiler_params=pltpu.CompilerParams(
+            collective_id=0, has_side_effects=True, vmem_limit_bytes=48 << 20
+        ),
+    )(slab, labels.reshape(1, -1), sample_rows, sample_count, slot_offset, centres)
+
+
 def solution(mesh):
+    n_p, n_f = mesh.shape["pts"], mesh.shape["feat"]
+
+    def body(slab, centres, labels, sample_rows, sample_count, slot_offset):
+        width = slab.shape[1]
+        slots = sample_rows.shape[2]
+        fits = (
+            width == LANES + HALF and n_f % 2 == 0 and 3 * n_p * slots <= LANES
+            and n_p * SUB <= LANES and 2 * slots <= SUB and centres.shape[0] % 512 == 0
+            and slab.shape[0] % (n_f * 512) == 0
+        )
+        args = (slab, centres, labels, sample_rows, sample_count, slot_offset)
+        return fused(n_p, n_f, *args) if fits else local(*args)
+
     placed = (
         P("pts", "feat"),
         P(),
@@ -54,5 +344,5 @@
         P("pts", None),
     )
     return jax.shard_map(
-        local, mesh=mesh, in_specs=placed, out_specs=P("pts", "feat"), check_vma=False
+        body, mesh=mesh, in_specs=placed, out_specs=P("pts", "feat"), check_vma=False
     )

time: 100 us -> 37 us (0.37)
  blocking collectives: 47.4 us -> 0 us
  Pallas kernels: 0 us -> 32 us
  other arithmetic: 15.9 us -> 0 us
  starting transfers between devices: 9.3 us -> 0 us
  local copies, waits for them, and re-layouts: 12.6 us -> 4.78 us
  matrix products: 7.52 us -> 0 us
  waiting for transfers between devices: 6.57 us -> 0 us
    psum x1 -> x0, blocking collectives: 42 us -> none  [local(): lax.psum((cost_part, size_part), ('pts', 'feat'))]
    pallas_call x0 -> x1, Pallas kernels: none -> 32 us  [fused(): pl.pallas_call(functools.partial(kernel, n_p, n_f, chunks, tile), out_sha...]
    all_to_all x2 -> x0, starting transfers between devices: 9.3 us -> none  [the longest x1 5.07 us: local(): lax.all_to_all(scaled, 'pts', split_axis=0, concat_axis=0, tiled=True)]
    gather x7 -> x0, local copies, waits for them, and re-layouts: 7.79 us -> none  [the longest x1 3.14 us: local(): jnp.take(cluster_size, member)]
    dot_general x1 -> x0, matrix products: 7.52 us -> none  [local(): lax.dot_general(points, centres, contract, preferred_element_type=jnp.flo...]
    scatter-add x3 -> x0, other arithmetic: 7.42 us -> none  [the longest x1 3.39 us: local(): jax.ops.segment_sum(jnp.ones_like(nearest), member, num_segments=centre_c...]
    all_to_all x2 -> x0, waiting for transfers between devices: 6.57 us -> none  [the longest x1 6.57 us: local(): lax.all_to_all(scaled, 'pts', split_axis=0, concat_axis=0, tiled=True)]
    all_gather x1 -> x0, blocking collectives: 5.45 us -> none  [local(): shard_sens = lax.all_gather(own_sens, 'feat', axis=0, tiled=True)]
  transfers between devices with their start and end apart: 2 -> 0, of which waited for: 1 -> 0; matrix products, arithmetic and copies ran while one was open for 14% -> 0% of each run, Pallas kernels for 0% -> 0%
where the time goes in v1:
time: 37 us; the launch traced here: 36.8 us
  Pallas kernels  32 us (86%)
  local copies, waits for them, and re-layouts  4.78 us (13%)
    pallas_call x1, Pallas kernels, fused(): pl.pallas_call(functools.partial(kernel, n_p, n_f, chunks, tile), out_sha...  32 us
    unnamed x9, local copies, waits for them, and re-layouts  4.78 us

profile of v1, /device:TPU:0, one launch (start us, length us, event | category | flops | bytes accessed | tf_op | source)
XLA Modules:
  0.0 36.8 jit_solution(6106544955036051945)
XLA Ops:
  0.0 0.8 %copy.8.rows_ref = s32[1,8,4]{2,1,0:T(8,128)S(1)} copy(s32[1,8,4]{1,2,0:T(4,128)} %param.9) | data formatting | bytes 256 | tf_op args[3]
  0.8 1.4 %copy.7.slab_ref = bf16[2048,192]{1,0:T(8,128)(2,1)S(1)} copy(bf16[2048,192]{0,1:T(8,128)(2,1)} %param.6) | data formatting | bytes 1572864 | tf_op args[0]
  2.2 0.0 copy-start
  2.2 0.7 %copy-done = s32[512,1]{0,1:T(1,128)S(1)} copy-done((s32[512,1]{0,1:T(1,128)S(1)}, s32[512,1]{0,1:T(1,128)}, u32[]{:S(2)}) %copy-start) | copy-done | bytes 2072
  2.9 0.0 copy-start.1
  2.9 0.7 %copy-done.1 = s32[1,8]{1,0:T(1,128)S(1)} copy-done((s32[1,8]{1,0:T(1,128)S(1)}, s32[1,8]{1,0:T(1,128)}, u32[]{:S(2)}) %copy-start.1) | copy-done | bytes 56
  3.5 0.0 copy-start.2
  3.5 0.7 %copy-done.2 = s32[1,8]{1,0:T(1,128)S(1)} copy-done((s32[1,8]{1,0:T(1,128)S(1)}, s32[1,8]{1,0:T(1,128)}, u32[]{:S(2)}) %copy-start.2) | copy-done | bytes 56
  4.2 32.0 %shard_map.64 = bf16[32,192]{1,0:T(8,128)(2,1)S(1)} custom-call(bf16[2048,192]{1,0:T(8,128)(2,1)S(1)} %copy.7.slab_ref, s32[1,512]{1,0:T(1,128)S(1)} %bitcast.1, s32[1,8,4]{2,1,0:T(8,128)S(1)} %copy.8.rows_ref, s32[1,8]{1,0:T(1,128)S(1)} %copy-done.1, s32[1,8]{1,0:T(1,128)S(1)} %copy-done.2, bf16[4096,768]{1,0:T(8,128)(2,1)} %cen_hbm.1), custom_call_target="tpu_custom_call" | custom-call | tf_op jit(solution)/shard_map/pallas_call | solution.py:293
  36.2 0.6 %copy.10 = bf16[32,192]{1,0:T(8,128)(2,1)} copy(bf16[32,192]{1,0:T(8,128)(2,1)S(1)} %shard_map.64) | data formatting | bytes 24576
Async XLA Ops:
  2.2 0.7 %copy-start = (s32[512,1]{0,1:T(1,128)S(1)}, s32[512,1]{0,1:T(1,128)}, u32[]{:S(2)}) copy-start(s32[512,1]{0,1:T(1,128)} %param.8) | copy-start | bytes 6148
  2.9 0.7 %copy-start.1 = (s32[1,8]{1,0:T(1,128)S(1)}, s32[1,8]{1,0:T(1,128)}, u32[]{:S(2)}) copy-start(s32[1,8]{1,0:T(1,128)} %count_ref.1) | copy-start | bytes 100
  3.5 0.7 %copy-start.2 = (s32[1,8]{1,0:T(1,128)S(1)}, s32[1,8]{1,0:T(1,128)}, u32[]{:S(2)}) copy-start(s32[1,8]{1,0:T(1,128)} %offset_ref.1) | copy-start | bytes 100

commit v2 on v1

--- a/solution.py
+++ b/solution.py
@@ -9,8 +9,9 @@
 
 NT = (((1,), (1,)), ((), ()))
 LANES = 128
-HALF = LANES // 2
 SUB = 8
+CHUNK = 256
+TILE = 512
 MESH = pl.DeviceIdType.MESH
 
 
@@ -53,18 +54,17 @@
     return placed.astype(jnp.bfloat16)
 
 
-def kernel(n_p, n_f, chunks, tile, slab_ref, labels_ref, rows_ref, count_ref, offset_ref, cen_hbm,
-           out_ref, cen, csq, pack_a, pack_b, got_a, got_b, lab_msg, lab_all, row_msg, row_all,
-           red_msg, red_all, cen_sem, a_send, a_recv, b_send, b_recv, lab_send, lab_recv,
-           row_send, row_recv, red_send, red_recv):
+def kernel(n_p, n_f, chunks, tile, slab_hbm, labels_hbm, rows_hbm, count_hbm, offset_hbm, cen_hbm,
+           out_ref, cen, csq, slab_ref, points_ref, labels_ref, rows_ref, count_ref, offset_ref,
+           lab_msg, lab_all, row_msg, row_all, red_msg, red_all, in_sem, cen_sem, a_send, a_recv,
+           lab_send, lab_recv, row_send, row_recv, red_send, red_recv):
     f32, bf16 = jnp.float32, jnp.bfloat16
-    rows_pts, width = slab_ref.shape
+    width, rows_pts = slab_ref.shape
     rows_dev = rows_pts // n_f
     crow = rows_dev // chunks
-    hrow = crow // 2
     n = n_p * n_f
     centre_count = cen.shape[0]
-    slots = rows_ref.shape[2]
+    slots = rows_ref.shape[1]
     tiles = centre_count // tile
     my_p, my_f = lax.axis_index("pts"), lax.axis_index("feat")
     me = my_p * n_f + my_f
@@ -77,29 +77,24 @@
     for d in range(1, n):
         pl.semaphore_signal(barrier, inc=1, device_id=device(d), device_id_type=MESH)
 
+    own_k = pl.ds(pl.multiple_of(my_f * width, width), width)
+    own_cols = pl.ds(pl.multiple_of(my_f * rows_dev, rows_dev), rows_dev)
+    in_copies = [
+        pltpu.make_async_copy(rows_hbm, rows_ref, in_sem.at[0]),
+        pltpu.make_async_copy(count_hbm, count_ref, in_sem.at[1]),
+        pltpu.make_async_copy(offset_hbm, offset_ref, in_sem.at[2]),
+        pltpu.make_async_copy(labels_hbm, labels_ref, in_sem.at[3]),
+        pltpu.make_async_copy(slab_hbm, slab_ref, in_sem.at[4]),
+        pltpu.make_async_copy(slab_hbm.at[:, own_cols], points_ref.at[own_k], in_sem.at[5]),
+    ]
+    for copy in in_copies:
+        copy.start()
     cen_copies = []
     for t in range(tiles):
         part = pl.ds(t * tile, tile)
         copy = pltpu.make_async_copy(cen_hbm.at[part], cen.at[part], cen_sem.at[t])
         copy.start()
         cen_copies.append(copy)
-
-    odd = lax.rem(my_f, 2)
-
-    @pl.loop(0, n_f * chunks)
-    def _(j):
-        base = pl.multiple_of(j * crow, crow)
-        left = slab_ref[pl.ds(base, crow), :LANES].astype(f32)
-        right = slab_ref[pl.ds(base, crow), LANES:width].astype(f32)
-        right = jnp.concatenate([right, right], axis=1)
-        turned = pltpu.roll(left, HALF, 1)
-        low = lax.broadcasted_iota(jnp.int32, (crow, LANES), 1) < HALF
-        is_odd = jnp.full((crow, LANES), odd, jnp.int32) == 1
-        main = jnp.where(is_odd, jnp.where(low, turned, right), left)
-        rest = jnp.where(is_odd, jnp.where(low, left, turned), right)
-        pack_a[pl.ds(base, crow), :] = main.astype(bf16)
-        both = jnp.where(low[:hrow], rest[:hrow], rest[hrow:])
-        pack_b[pl.ds(pl.multiple_of(j * hrow, hrow), hrow), :] = both.astype(bf16)
 
     pl.semaphore_wait(barrier, n - 1)
 
@@ -110,27 +105,23 @@
         for e in order:
             peer = lax.rem(my_f + e, n_f)
             at = pl.multiple_of(peer * rows_dev + c * crow, crow)
-            half_at = pl.multiple_of(peer * (rows_dev // 2) + c * hrow, hrow)
             copies.append(pltpu.make_async_remote_copy(
-                src_ref=pack_a.at[pl.ds(at, crow)], dst_ref=got_a.at[my_f, pl.ds(c * crow, crow)],
+                src_ref=slab_hbm.at[:, pl.ds(at, crow)],
+                dst_ref=points_ref.at[own_k, pl.ds(c * crow, crow)],
                 send_sem=a_send.at[c, e - 1], recv_sem=a_recv.at[c, e - 1],
-                device_id=(my_p, peer), device_id_type=MESH))
-            copies.append(pltpu.make_async_remote_copy(
-                src_ref=pack_b.at[pl.ds(half_at, hrow)], dst_ref=got_b.at[my_f, pl.ds(c * hrow, hrow)],
-                send_sem=b_send.at[c, e - 1], recv_sem=b_recv.at[c, e - 1],
                 device_id=(my_p, peer), device_id_type=MESH))
         for copy in copies:
             copy.start()
         slab_copies.append(copies)
-    got_a[my_f] = pack_a[pl.ds(pl.multiple_of(my_f * rows_dev, rows_dev), rows_dev), :]
-    got_b[my_f] = pack_b[pl.ds(pl.multiple_of(my_f * (rows_dev // 2), rows_dev // 2), rows_dev // 2), :]
+    for copy in in_copies:
+        copy.wait()
 
     queries = n_p * SUB
     query_sub = lax.broadcasted_iota(jnp.int32, (queries, 1), 0)
     picked = jnp.full((queries, 1), -1, jnp.int32)
     for o in range(n_p):
         for s in range(slots):
-            picked = jnp.where(query_sub == o * SUB + s, rows_ref[0, o, s], picked)
+            picked = jnp.where(query_sub == o * SUB + s, rows_ref[0, s, o], picked)
     members = labels_ref[...].astype(f32)
     lane_dev = lax.broadcasted_iota(jnp.int32, (queries, rows_dev), 1)
     own_hit = (lane_dev + my_f * rows_dev) == picked
@@ -151,7 +142,7 @@
 
     lane_pts = lax.broadcasted_iota(jnp.int32, (queries, rows_pts), 1)
     chosen = jnp.where(lane_pts == picked, 1.0, 0.0).astype(bf16)
-    chosen = jnp.dot(chosen, slab_ref[...], preferred_element_type=f32)
+    chosen = lax.dot_general(chosen, slab_ref[...], NT, preferred_element_type=f32)
     live = jnp.zeros((queries, 1), f32)
     for o in range(n_p):
         for s in range(slots):
@@ -199,33 +190,17 @@
         size = jnp.sum(jnp.where(want == members, 1.0, 0.0), axis=1, keepdims=True)
         sums = jnp.where(is_slot & (lanes == span + p * slots + slot), size, sums)
 
-    ones = jnp.ones((SUB, cen.shape[1]), bf16)
     near_parts = []
     for c in range(chunks):
         for copy in slab_copies[c]:
             copy.wait_recv()
-        rows = pl.ds(c * crow, crow)
-        half_rows = pl.ds(c * hrow, hrow)
-        low = lax.broadcasted_iota(jnp.int32, (hrow, LANES), 1) < HALF
-        blocks = []
-        for pair in range(n_f // 2):
-            even_b = got_b[2 * pair, half_rows].astype(f32)
-            odd_b = got_b[2 * pair + 1, half_rows].astype(f32)
-            top = jnp.where(low, even_b, pltpu.roll(odd_b, HALF, 1))
-            bottom = jnp.where(low, pltpu.roll(even_b, HALF, 1), odd_b)
-            middle = jnp.concatenate([top, bottom], axis=0).astype(bf16)
-            blocks += [got_a[2 * pair, rows], middle, got_a[2 * pair + 1, rows]]
-        points = jnp.concatenate(blocks, axis=1)
+        points = points_ref[:, c * crow:(c + 1) * crow]
         wide = points.astype(f32)
-        wide = wide * wide
-        high = wide.astype(bf16)
-        rest = (wide - high.astype(f32)).astype(bf16)
-        point_sq = (lax.dot_general(ones, high, NT, preferred_element_type=f32)
-                    + lax.dot_general(ones, rest, NT, preferred_element_type=f32))[:1]
+        point_sq = jnp.sum(wide * wide, axis=0, keepdims=True)
 
         def step(t, best):
             part = pl.ds(pl.multiple_of(t * tile, tile), tile)
-            cross = lax.dot_general(cen[part, :], points, NT, preferred_element_type=f32)
+            cross = jnp.dot(cen[part, :], points, preferred_element_type=f32)
             square = csq[part, :]
             gap = jnp.concatenate([square] * (crow // LANES), axis=1) - 2.0 * cross
             return jnp.minimum(best, jnp.min(gap.reshape(tile // SUB, SUB, crow), axis=0))
@@ -283,54 +258,52 @@
     rows_dev = rows_pts // n_f
     centre_count, depth = centres.shape
     slots = sample_rows.shape[2]
-    chunks = 2
-    tile = 512
-    tiles = centre_count // tile
+    chunks = rows_dev // CHUNK
+    tiles = centre_count // TILE
     n = n_p * n_f
     wide = pl.cdiv(width, LANES) * LANES
-    vmem, smem = pl.BlockSpec(memory_space=pltpu.VMEM), pl.BlockSpec(memory_space=pltpu.SMEM)
+    rows_in = sample_rows.transpose(0, 2, 1)
+    labels_in = labels.reshape(1, -1)
     dma = pltpu.SemaphoreType.DMA
     return pl.pallas_call(
-        functools.partial(kernel, n_p, n_f, chunks, tile),
+        functools.partial(kernel, n_p, n_f, chunks, TILE),
         out_shape=jax.ShapeDtypeStruct((n_p * slots, width), jnp.bfloat16),
-        in_specs=[vmem, vmem, smem, smem, smem, pl.BlockSpec(memory_space=pl.ANY)],
-        out_specs=vmem,
+        in_specs=[pl.BlockSpec(memory_space=pl.ANY)] * 6,
+        out_specs=pl.BlockSpec(memory_space=pltpu.VMEM),
         scratch_shapes=[
             pltpu.VMEM((centre_count, depth), jnp.bfloat16),
             pltpu.VMEM((centre_count, LANES), jnp.float32),
-            pltpu.VMEM((rows_pts, LANES), jnp.bfloat16),
-            pltpu.VMEM((rows_pts // 2, LANES), jnp.bfloat16),
-            pltpu.VMEM((n_f, rows_dev, LANES), jnp.bfloat16),
-            pltpu.VMEM((n_f, rows_dev // 2, LANES), jnp.bfloat16),
+            pltpu.VMEM((width, rows_pts), jnp.bfloat16),
+            pltpu.VMEM((depth, rows_dev), jnp.bfloat16),
+            pltpu.VMEM(labels_in.shape, jnp.int32),
+            pltpu.SMEM(rows_in.shape, jnp.int32),
+            pltpu.SMEM(sample_count.shape, jnp.int32),
+            pltpu.SMEM(slot_offset.shape, jnp.int32),
             pltpu.VMEM((1, LANES), jnp.float32),
             pltpu.VMEM((n, 1, LANES), jnp.float32),
             pltpu.VMEM((n_p, SUB, wide), jnp.float32),
             pltpu.VMEM((n_p, SUB, wide), jnp.float32),
             pltpu.VMEM((n_p, 1, LANES), jnp.float32),
             pltpu.VMEM((n, 1, LANES), jnp.float32),
-            dma((tiles,)),
-            dma((chunks, n_f - 1)), dma((chunks, n_f - 1)),
+            dma((6,)), dma((tiles,)),
             dma((chunks, n_f - 1)), dma((chunks, n_f - 1)),
             dma((n - 1,)), dma((n - 1,)),
             dma((n_p - 1,)), dma((n_p - 1,)),
             dma((n - 1,)), dma((n - 1,)),
         ],
-        compiler_params=pltpu.CompilerParams(
-            collective_id=0, has_side_effects=True, vmem_limit_bytes=48 << 20
-        ),
-    )(slab, labels.reshape(1, -1), sample_rows, sample_count, slot_offset, centres)
+        compiler_params=pltpu.CompilerParams(collective_id=0, has_side_effects=True),
+    )(slab.T, labels_in, rows_in, sample_count, slot_offset, centres)
 
 
 def solution(mesh):
     n_p, n_f = mesh.shape["pts"], mesh.shape["feat"]
 
     def body(slab, centres, labels, sample_rows, sample_count, slot_offset):
-        width = slab.shape[1]
+        rows_dev = slab.shape[0] // n_f
         slots = sample_rows.shape[2]
         fits = (
-            width == LANES + HALF and n_f % 2 == 0 and 3 * n_p * slots <= LANES
-            and n_p * SUB <= LANES and 2 * slots <= SUB and centres.shape[0] % 512 == 0
-            and slab.shape[0] % (n_f * 512) == 0
+            slab.shape[1] % 16 == 0 and rows_dev % CHUNK == 0 and centres.shape[0] % TILE == 0
+            and 3 * n_p * slots <= LANES and n_p * SUB <= LANES and 2 * slots <= SUB
         )
         args = (slab, centres, labels, sample_rows, sample_count, slot_offset)
         return fused(n_p, n_f, *args) if fits else local(*args)

time: 37 us -> 32.3 us (0.87)
  local copies, waits for them, and re-layouts: 4.78 us -> 1.32 us
  Pallas kernels: 32 us -> 30.8 us
    unnamed x9 -> x1, local copies, waits for them, and re-layouts: 4.78 us -> 1.32 us
    pallas_call x1, Pallas kernels: 32 us -> 30.8 us  [fused(): pl.pallas_call(functools.partial(kernel, n_p, n_f, chunks, TILE), out_sha...]
where the time goes in v2:
time: 32.3 us; the launch traced here: 32.1 us
  Pallas kernels  30.8 us (95%)
  local copies, waits for them, and re-layouts  1.32 us (4%)
    pallas_call x1, Pallas kernels, fused(): pl.pallas_call(functools.partial(kernel, n_p, n_f, chunks, TILE), out_sha...  30.8 us
    unnamed x1, local copies, waits for them, and re-layouts  1.32 us

profile of v2, /device:TPU:0, one launch (start us, length us, event | category | flops | bytes accessed | tf_op | source)
XLA Modules:
  0.0 32.1 jit_solution(16178839703622670246)
XLA Ops:
  0.0 30.8 %shard_map.64 = bf16[32,192]{1,0:T(8,128)(2,1)} custom-call(bf16[192,2048]{1,0:T(8,128)(2,1)} %bitcast.3, s32[1,512]{1,0:T(1,128)} %bitcast.4, s32[1,4,8]{2,1,0:T(4,128)} %bitcast.5, s32[1,8]{1,0:T(1,128)} %count_hbm.1, s32[1,8]{1,0:T(1,128)} %offset_hbm.1, bf16[4096,768]{1,0:T(8,128)(2,1)} %cen_hbm.1), custom_call_target="tpu_custom_call" | custom-call | tf_op jit(solution)/shard_map/pallas_call | solution.py:268
  30.8 1.3 %copy.8 = bf16[32,192]{1,0:T(8,128)(2,1)} copy(bf16[32,192]{1,0:T(8,128)(2,1)} %shard_map.64) | data formatting | bytes 24576

commit v3 on v2

--- a/solution.py
+++ b/solution.py
@@ -96,7 +96,34 @@
         copy.start()
         cen_copies.append(copy)
 
+    for copy in in_copies[:4]:
+        copy.wait()
+
+    queries = n_p * SUB
+    query_sub = lax.broadcasted_iota(jnp.int32, (queries, 1), 0)
+    picked = jnp.full((queries, 1), -1, jnp.int32)
+    for o in range(n_p):
+        for s in range(slots):
+            picked = jnp.where(query_sub == o * SUB + s, rows_ref[0, s, o], picked)
+    members = labels_ref[...].astype(f32)
+    lane_dev = lax.broadcasted_iota(jnp.int32, (queries, rows_dev), 1)
+    own_hit = (lane_dev + my_f * rows_dev) == picked
+    own_label = jnp.sum(jnp.where(own_hit, members + 1.0, 0.0), axis=1, keepdims=True)
+    query_diag = (lax.broadcasted_iota(jnp.int32, (queries, LANES), 0)
+                  == lax.broadcasted_iota(jnp.int32, (queries, LANES), 1))
+    label_row = jnp.sum(jnp.where(query_diag, own_label, 0.0), axis=0, keepdims=True)
+    lab_msg[...] = label_row
+    lab_all[me] = label_row
+
     pl.semaphore_wait(barrier, n - 1)
+
+    lab_copies = []
+    for d in range(1, n):
+        copy = pltpu.make_async_remote_copy(
+            src_ref=lab_msg, dst_ref=lab_all.at[me], send_sem=lab_send.at[d - 1],
+            recv_sem=lab_recv.at[d - 1], device_id=device(d), device_id_type=MESH)
+        copy.start()
+        lab_copies.append(copy)
 
     slab_copies = []
     order = [e for e in range(2, n_f)] + [1]
@@ -113,32 +140,8 @@
         for copy in copies:
             copy.start()
         slab_copies.append(copies)
-    for copy in in_copies:
-        copy.wait()
-
-    queries = n_p * SUB
-    query_sub = lax.broadcasted_iota(jnp.int32, (queries, 1), 0)
-    picked = jnp.full((queries, 1), -1, jnp.int32)
-    for o in range(n_p):
-        for s in range(slots):
-            picked = jnp.where(query_sub == o * SUB + s, rows_ref[0, s, o], picked)
-    members = labels_ref[...].astype(f32)
-    lane_dev = lax.broadcasted_iota(jnp.int32, (queries, rows_dev), 1)
-    own_hit = (lane_dev + my_f * rows_dev) == picked
-    own_label = jnp.sum(jnp.where(own_hit, members + 1.0, 0.0), axis=1, keepdims=True)
-    query_diag = (lax.broadcasted_iota(jnp.int32, (queries, LANES), 0)
-                  == lax.broadcasted_iota(jnp.int32, (queries, LANES), 1))
-    label_row = jnp.sum(jnp.where(query_diag, own_label, 0.0), axis=0, keepdims=True)
-    lab_msg[...] = label_row
-    lab_all[me] = label_row
-
-    lab_copies = []
-    for d in range(1, n):
-        copy = pltpu.make_async_remote_copy(
-            src_ref=lab_msg, dst_ref=lab_all.at[me], send_sem=lab_send.at[d - 1],
-            recv_sem=lab_recv.at[d - 1], device_id=device(d), device_id_type=MESH)
-        copy.start()
-        lab_copies.append(copy)
+    for copy in in_copies[4:]:
+        copy.wait()
 
     lane_pts = lax.broadcasted_iota(jnp.int32, (queries, rows_pts), 1)
     chosen = jnp.where(lane_pts == picked, 1.0, 0.0).astype(bf16)

time: 32.3 us -> 27.5 us (0.85)
  Pallas kernels: 30.8 us -> 25.9 us
    pallas_call x1, Pallas kernels: 30.8 us -> 25.9 us  [fused(): pl.pallas_call(functools.partial(kernel, n_p, n_f, chunks, TILE), out_sha...]
where the time goes in v3:
time: 27.5 us; the launch traced here: 27.3 us
  Pallas kernels  25.9 us (94%)
  local copies, waits for them, and re-layouts  1.32 us (5%)
    pallas_call x1, Pallas kernels, fused(): pl.pallas_call(functools.partial(kernel, n_p, n_f, chunks, TILE), out_sha...  25.9 us
    unnamed x1, local copies, waits for them, and re-layouts  1.32 us

profile of v3, /device:TPU:0, one launch (start us, length us, event | category | flops | bytes accessed | tf_op | source)
XLA Modules:
  0.0 27.3 jit_solution(12930785595669243418)
XLA Ops:
  0.0 25.9 %shard_map.64 = bf16[32,192]{1,0:T(8,128)(2,1)} custom-call(bf16[192,2048]{1,0:T(8,128)(2,1)} %bitcast.3, s32[1,512]{1,0:T(1,128)} %bitcast.4, s32[1,4,8]{2,1,0:T(4,128)} %bitcast.5, s32[1,8]{1,0:T(1,128)} %count_hbm.1, s32[1,8]{1,0:T(1,128)} %offset_hbm.1, bf16[4096,768]{1,0:T(8,128)(2,1)} %cen_hbm.1), custom_call_target="tpu_custom_call" | custom-call | tf_op jit(solution)/shard_map/pallas_call | solution.py:271
  25.9 1.3 %copy.8 = bf16[32,192]{1,0:T(8,128)(2,1)} copy(bf16[32,192]{1,0:T(8,128)(2,1)} %shard_map.64) | data formatting | bytes 24576

commit v4 on v2

--- a/solution.py
+++ b/solution.py
@@ -11,7 +11,7 @@
 LANES = 128
 SUB = 8
 CHUNK = 256
-TILE = 512
+TILE = 2048
 MESH = pl.DeviceIdType.MESH
 
 
@@ -55,7 +55,7 @@
 
 
 def kernel(n_p, n_f, chunks, tile, slab_hbm, labels_hbm, rows_hbm, count_hbm, offset_hbm, cen_hbm,
-           out_ref, cen, csq, slab_ref, points_ref, labels_ref, rows_ref, count_ref, offset_ref,
+           out_ref, cen, csq, gap_ref, slab_ref, points_ref, labels_ref, rows_ref, count_ref, offset_ref,
            lab_msg, lab_all, row_msg, row_all, red_msg, red_all, in_sem, cen_sem, a_send, a_recv,
            lab_send, lab_recv, row_send, row_recv, red_send, red_recv):
     f32, bf16 = jnp.float32, jnp.bfloat16
@@ -98,22 +98,24 @@
 
     pl.semaphore_wait(barrier, n - 1)
 
+    odd = lax.rem(my_f, 2)
+    partner = my_f + 1 - 2 * odd
+    peers = [partner, lax.rem(my_f + 2, n_f), lax.rem(partner + 2, n_f)]
     slab_copies = []
-    order = [e for e in range(2, n_f)] + [1]
     for c in range(chunks):
         copies = []
-        for e in order:
-            peer = lax.rem(my_f + e, n_f)
+        for r, peer in enumerate(peers):
             at = pl.multiple_of(peer * rows_dev + c * crow, crow)
             copies.append(pltpu.make_async_remote_copy(
                 src_ref=slab_hbm.at[:, pl.ds(at, crow)],
                 dst_ref=points_ref.at[own_k, pl.ds(c * crow, crow)],
-                send_sem=a_send.at[c, e - 1], recv_sem=a_recv.at[c, e - 1],
+                send_sem=a_send.at[c, r], recv_sem=a_recv.at[c, r],
                 device_id=(my_p, peer), device_id_type=MESH))
-        for copy in copies:
-            copy.start()
         slab_copies.append(copies)
-    for copy in in_copies:
+    for copy in slab_copies[0][1:] + slab_copies[0][:1]:
+        copy.start()
+
+    for copy in in_copies[:4]:
         copy.wait()
 
     queries = n_p * SUB
@@ -132,6 +134,7 @@
     lab_msg[...] = label_row
     lab_all[me] = label_row
 
+
     lab_copies = []
     for d in range(1, n):
         copy = pltpu.make_async_remote_copy(
@@ -139,6 +142,12 @@
             recv_sem=lab_recv.at[d - 1], device_id=device(d), device_id_type=MESH)
         copy.start()
         lab_copies.append(copy)
+
+    for copies in slab_copies[1:]:
+        for copy in copies[1:] + copies[:1]:
+            copy.start()
+    for copy in in_copies[4:]:
+        copy.wait()
 
     lane_pts = lax.broadcasted_iota(jnp.int32, (queries, rows_pts), 1)
     chosen = jnp.where(lane_pts == picked, 1.0, 0.0).astype(bf16)
@@ -173,6 +182,35 @@
             total += piece * piece
         csq[part, :] = jnp.broadcast_to(jnp.sum(total, axis=1, keepdims=True), (tile, LANES))
 
+    start = jnp.full((SUB, crow), jnp.inf, f32)
+
+    def part_of(t):
+        return pl.ds(pl.multiple_of(t * tile, tile), tile)
+
+    def lower(best, gap):
+        return jnp.minimum(best, jnp.min(gap.reshape(tile // SUB, SUB, crow), axis=0))
+
+    def squares(part):
+        return jnp.concatenate([csq[part, :]] * (crow // LANES), axis=1)
+
+    def finish(best, cols):
+        wide = points_ref[:, cols].astype(f32)
+        return jnp.sum(wide * wide, axis=0, keepdims=True) + jnp.min(best, axis=0, keepdims=True)
+
+    near_parts = []
+    for c in range(chunks - 1):
+        for copy in slab_copies[c]:
+            copy.wait_recv()
+        cols = pl.ds(c * crow, crow)
+        points = points_ref[:, cols]
+
+        def step(t, best):
+            part = part_of(t)
+            cross = jnp.dot(cen[part, :], points, preferred_element_type=f32)
+            return lower(best, squares(part) - 2.0 * cross)
+
+        near_parts.append(finish(lax.fori_loop(0, tiles, step, start), cols))
+
     for copy in lab_copies:
         copy.wait()
     lanes = lax.broadcasted_iota(jnp.int32, (queries, LANES), 1)
@@ -190,23 +228,34 @@
         size = jnp.sum(jnp.where(want == members, 1.0, 0.0), axis=1, keepdims=True)
         sums = jnp.where(is_slot & (lanes == span + p * slots + slot), size, sums)
 
-    near_parts = []
-    for c in range(chunks):
-        for copy in slab_copies[c]:
-            copy.wait_recv()
-        points = points_ref[:, c * crow:(c + 1) * crow]
-        wide = points.astype(f32)
-        point_sq = jnp.sum(wide * wide, axis=0, keepdims=True)
-
-        def step(t, best):
-            part = pl.ds(pl.multiple_of(t * tile, tile), tile)
-            cross = jnp.dot(cen[part, :], points, preferred_element_type=f32)
-            square = csq[part, :]
-            gap = jnp.concatenate([square] * (crow // LANES), axis=1) - 2.0 * cross
-            return jnp.minimum(best, jnp.min(gap.reshape(tile // SUB, SUB, crow), axis=0))
-
-        best = lax.fori_loop(0, tiles, step, jnp.full((SUB, crow), jnp.inf, f32))
-        near_parts.append(point_sq + jnp.min(best, axis=0, keepdims=True))
+    pair = 2 * width
+    last = pl.cdiv(width, LANES) * LANES
+    here = my_f // 2
+    away = 1 - here
+    cols = pl.ds((chunks - 1) * crow, crow)
+    here_k = pl.ds(pl.multiple_of(here * pair, LANES), pair)
+    lone_k = pl.ds(pl.multiple_of(away * pair + odd * last, LANES), pair - last)
+    last_k = pl.ds(pl.multiple_of(away * pair + (1 - odd) * (pair - last), LANES), last)
+    for copy in slab_copies[-1][:2]:
+        copy.wait_recv()
+    first = jnp.concatenate([points_ref[here_k, cols], points_ref[lone_k, cols]], axis=0)
+
+    @pl.loop(0, tiles)
+    def _(t):
+        part = part_of(t)
+        mine = jnp.concatenate([cen[part, here_k], cen[part, lone_k]], axis=1)
+        cross = jnp.dot(mine, first, preferred_element_type=f32)
+        gap_ref[part, :] = squares(part) - 2.0 * cross
+
+    slab_copies[-1][2].wait_recv()
+    final = points_ref[last_k, cols]
+
+    def last_step(t, best):
+        part = part_of(t)
+        cross = jnp.dot(cen[part, last_k], final, preferred_element_type=f32)
+        return lower(best, gap_ref[part, :] - 2.0 * cross)
+
+    near_parts.append(finish(lax.fori_loop(0, tiles, last_step, start), cols))
     nearest = jnp.concatenate(near_parts, axis=1)
 
     for p in range(n_p):
@@ -273,6 +322,7 @@
         scratch_shapes=[
             pltpu.VMEM((centre_count, depth), jnp.bfloat16),
             pltpu.VMEM((centre_count, LANES), jnp.float32),
+            pltpu.VMEM((centre_count, CHUNK), jnp.float32),
             pltpu.VMEM((width, rows_pts), jnp.bfloat16),
             pltpu.VMEM((depth, rows_dev), jnp.bfloat16),
             pltpu.VMEM(labels_in.shape, jnp.int32),
@@ -303,6 +353,7 @@
         slots = sample_rows.shape[2]
         fits = (
             slab.shape[1] % 16 == 0 and rows_dev % CHUNK == 0 and centres.shape[0] % TILE == 0
+            and n_f == 4 and 2 * slab.shape[1] % LANES == 0 and slab.shape[1] > LANES and rows_dev // CHUNK > 1
             and 3 * n_p * slots <= LANES and n_p * SUB <= LANES and 2 * slots <= SUB
         )
         args = (slab, centres, labels, sample_rows, sample_count, slot_offset)

time: 32.3 us -> 25.7 us (0.80)
  Pallas kernels: 30.8 us -> 24.1 us
    pallas_call x1, Pallas kernels: 30.8 us -> 24.1 us  [fused(): pl.pallas_call(functools.partial(kernel, n_p, n_f, chunks, TILE), out_sha...]
where the time goes in v4:
time: 25.7 us; the launch traced here: 25.4 us
  Pallas kernels  24.1 us (94%)
  local copies, waits for them, and re-layouts  1.32 us (5%)
    pallas_call x1, Pallas kernels, fused(): pl.pallas_call(functools.partial(kernel, n_p, n_f, chunks, TILE), out_sha...  24.1 us
    unnamed x1, local copies, waits for them, and re-layouts  1.32 us

profile of v4, /device:TPU:0, one launch (start us, length us, event | category | flops | bytes accessed | tf_op | source)
XLA Modules:
  0.0 25.4 jit_solution(2601662733924661896)
XLA Ops:
  0.0 24.1 %shard_map.64 = bf16[32,192]{1,0:T(8,128)(2,1)} custom-call(bf16[192,2048]{1,0:T(8,128)(2,1)} %bitcast.3, s32[1,512]{1,0:T(1,128)} %bitcast.4, s32[1,4,8]{2,1,0:T(4,128)} %bitcast.5, s32[1,8]{1,0:T(1,128)} %count_hbm.1, s32[1,8]{1,0:T(1,128)} %offset_hbm.1, bf16[4096,768]{1,0:T(8,128)(2,1)} %cen_hbm.1), custom_call_target="tpu_custom_call" | custom-call | tf_op jit(solution)/shard_map/pallas_call | solution.py:317
  24.1 1.3 %copy.8 = bf16[32,192]{1,0:T(8,128)(2,1)} copy(bf16[32,192]{1,0:T(8,128)(2,1)} %shard_map.64) | data formatting | bytes 24576
